TPU v7x, 32 devices: a whole 2x2x4 slice. The times are simulated.
32 devices in a mesh: vis: 4 (over y, core), row: 4 (over z), col: 2 (over x).
Axes of the slice: x: 2, y: 2, z: 4, core: 2. Of those that a mesh axis runs over, the one named last changes fastest.
Arguments:
- images: bfloat16 [128, 6400], P(('vis', 'row', 'col')), may hold values from -6 to 6
- counts: int32 [4], replicated, may hold values from 1 to 32, 64 in all
- block_order: int32 [4], replicated, may hold values from 0 to 3, each once
- projector_norm_gain: float32 [6400], replicated, may hold values from 0.1 to 1.9
- proj_first: bfloat16 [6400, 4096], P('vis', ('row', 'col')), may hold values from -0.078125 to 0.078125
- proj_bias: float32 [4096], P(('row', 'col')), may hold values from -3 to 3
- proj_second: bfloat16 [4096, 4096], P(('row', 'col'), 'vis'), may hold values from -0.09375 to 0.09375
- gate_weight: bfloat16 [4096, 16384], P('vis', ('row', 'col')), may hold values from -0.09375 to 0.09375
- up_weight: bfloat16 [4096, 16384], P('vis', ('row', 'col')), may hold values from -0.09375 to 0.09375
- down_weight: bfloat16 [16384, 4096], P(('row', 'col'), 'vis'), may hold values from -0.046875 to 0.046875
- cotangent: bfloat16 [64, 4096], P(('row', 'col'), 'vis'), may hold values from -6 to 6
Outputs:
- block_out: bfloat16 [64, 4096], P(('row', 'col'), 'vis')
- image_slot_gradients: float32 [128, 6400], P(('vis', 'row', 'col'))
- first_grad: float32 [6400, 4096], P('vis', ('row', 'col'))
- second_grad: float32 [4096, 4096], P(('row', 'col'), 'vis')
Inputs may be any that keep to these rules, and one draw needn't show every extreme that they name: Vision device v's live rows are its first counts[v] slots; the counts sum to 64, and some device's slots are all live. `block_order`: each vision device's index once: the order in which the devices' live rows follow one another among the language rows.
All inputs are finite; a program needn't handle non-finite values.
Results may differ from a plain program's by a relative error of at most 0.034.
Values may be sent and summed in bfloat16 or wider, within the bound.
A program may use at most 64 MiB of HBM per device.

v0:
```python
import jax
import jax.numpy as jnp
from jax import lax
from jax.sharding import PartitionSpec as P


def row_tables(counts, block_order, total_rows, per_device, group_size):
    vision = counts.shape[0]
    labels = jnp.arange(vision, dtype=jnp.int32)
    chosen = (block_order[:, None] == labels[None, :]).astype(jnp.int32)
    ordered = jnp.sum(chosen * counts[None, :], axis=1)
    block_ends = jnp.cumsum(ordered)
    block_starts = block_ends - ordered
    language = jnp.arange(total_rows, dtype=jnp.int32)
    block_of = jnp.sum((block_ends[None, :] <= language[:, None]).astype(jnp.int32), axis=1)
    picked = (block_of[:, None] == labels[None, :]).astype(jnp.int32)
    owner = jnp.sum(picked * block_order[None, :], axis=1)
    offset = language - jnp.sum(picked * block_starts[None, :], axis=1)
    stride = vision * per_device
    source = offset // per_device * stride + owner * per_device + offset % per_device
    slots = jnp.arange(stride * group_size, dtype=jnp.int32)
    within = slots % stride
    slot_owner = within // per_device
    slot_offset = slots // stride * per_device + within % per_device
    owner_start = jnp.sum(chosen * block_starts[:, None], axis=0)
    matched = (slot_owner[:, None] == labels[None, :]).astype(jnp.int32)
    start_of = jnp.sum(matched * owner_start[None, :], axis=1)
    count_of = jnp.sum(matched * counts[None, :], axis=1)
    live = slot_offset < count_of
    target = jnp.where(live, start_of + slot_offset, 0)
    return (source, target, live)


def gelu_parts(pre):
    normal_cdf = 0.5 * (1.0 + jax.scipy.special.erf(pre * 0.7071067811865476))
    density = jnp.exp(-0.5 * pre * pre) * 0.3989422804014327
    return (pre * normal_cdf, normal_cdf + pre * density)


def apply_layer_norm(images, projector_norm_gain):
    values = images.astype(jnp.float32)
    mean_removed = values - jnp.mean(values, axis=-1, keepdims=True)
    variance = jnp.mean(mean_removed * mean_removed, axis=-1, keepdims=True)
    inverse_scale = lax.rsqrt(variance + 1e-05)
    standardized_input = mean_removed * inverse_scale
    return (
        standardized_input,
        inverse_scale,
        (standardized_input * projector_norm_gain).astype(jnp.bfloat16),
    )


def norm_gradient_pass(gradient_tuple, standardized_input, inverse_scale, projector_norm_gain):
    gain_scaled = gradient_tuple * projector_norm_gain
    return inverse_scale * (
        gain_scaled
        - jnp.mean(gain_scaled, axis=-1, keepdims=True)
        - standardized_input * jnp.mean(gain_scaled * standardized_input, axis=-1, keepdims=True)
    )


def product(left, right):
    return jnp.dot(left, right, preferred_element_type=jnp.float32)


def feed_grads(hidden_grad, gate_sum, up_sum, gate_sigmoid):
    gate_grad = (
        hidden_grad * up_sum * gate_sigmoid * (1.0 + gate_sum * (1.0 - gate_sigmoid))
    ).astype(jnp.bfloat16)
    up_grad = (hidden_grad * gate_sum * gate_sigmoid).astype(jnp.bfloat16)
    return (gate_grad, up_grad)


def on_device(
    images,
    counts,
    block_order,
    projector_norm_gain,
    proj_first,
    proj_bias,
    proj_second,
    gate_weight,
    up_weight,
    down_weight,
    cotangent,
):
    group_size = lax.axis_size(("row", "col"))
    per_device = images.shape[0]
    local_rows = cotangent.shape[0]
    total_rows = local_rows * group_size
    position = lax.axis_index(("row", "col"))
    source, target, live = row_tables(counts, block_order, total_rows, per_device, group_size)
    standardized_input, inverse_scale, norm_output = apply_layer_norm(images, projector_norm_gain)
    columns = lax.all_to_all(norm_output, "vis", split_axis=1, concat_axis=0, tiled=True)
    gathered = lax.all_gather(columns, ("row", "col"), axis=0, tiled=True)
    first_part = jnp.take(product(gathered, proj_first), source, axis=0)
    pre = lax.psum(first_part.astype(jnp.bfloat16), "vis").astype(jnp.float32) + proj_bias
    activated, slope = gelu_parts(pre)
    hidden_proj = activated.astype(jnp.bfloat16)
    inputs = lax.psum(product(hidden_proj, proj_second).astype(jnp.bfloat16), ("row", "col"))
    gate_part = product(inputs, gate_weight)
    up_part = product(inputs, up_weight)
    gate_sum, up_sum = (
        lax.psum(gate_part.astype(jnp.bfloat16), "vis").astype(jnp.float32),
        lax.psum(up_part.astype(jnp.bfloat16), "vis").astype(jnp.float32),
    )
    gate_sigmoid = jax.nn.sigmoid(gate_sum)
    hidden = (gate_sum * gate_sigmoid * up_sum).astype(jnp.bfloat16)
    block_part = lax.psum_scatter(
        product(hidden, down_weight).astype(jnp.bfloat16),
        ("row", "col"),
        scatter_dimension=0,
        tiled=True,
    ).astype(jnp.float32)
    own_inputs = lax.dynamic_slice_in_dim(inputs, position * local_rows, local_rows, 0)
    block_out = (own_inputs.astype(jnp.float32) + block_part).astype(jnp.bfloat16)
    upstream = lax.all_gather(cotangent, ("row", "col"), axis=0, tiled=True)
    hidden_part = product(upstream, down_weight.T)
    hidden_grad = lax.psum(hidden_part.astype(jnp.bfloat16), "vis").astype(jnp.float32)
    gate_grad, up_grad = feed_grads(hidden_grad, gate_sum, up_sum, gate_sigmoid)
    input_part = product(gate_grad, gate_weight.T) + product(up_grad, up_weight.T)
    input_grad = (
        upstream.astype(jnp.float32)
        + lax.psum(input_part.astype(jnp.bfloat16), ("row", "col")).astype(jnp.float32)
    ).astype(jnp.bfloat16)
    second_grad = product(hidden_proj.T, input_grad)
    pre_part = product(input_grad, proj_second.T)
    pre_grad = lax.psum(pre_part.astype(jnp.bfloat16), "vis").astype(jnp.float32)
    act_grad = (pre_grad * slope).astype(jnp.bfloat16)
    slot_act = jnp.where(
        live[:, None], jnp.take(act_grad, target, axis=0), jnp.zeros((), jnp.bfloat16)
    )
    first_grad = product(gathered.T, slot_act)
    slot_part = lax.psum_scatter(
        product(slot_act, proj_first.T).astype(jnp.bfloat16),
        ("row", "col"),
        scatter_dimension=0,
        tiled=True,
    ).astype(jnp.float32)
    return_values = lax.all_to_all(slot_part, "vis", split_axis=0, concat_axis=1, tiled=True)
    image_slot_gradients = norm_gradient_pass(
        return_values, standardized_input, inverse_scale, projector_norm_gain
    )
    return (block_out, image_slot_gradients, first_grad, second_grad)


def solution(mesh):
    in_specs = (
        P(("vis", "row", "col"), None),
        P(),
        P(),
        P(),
        P("vis", ("row", "col")),
        P(("row", "col")),
        P(("row", "col"), "vis"),
        P("vis", ("row", "col")),
        P("vis", ("row", "col")),
        P(("row", "col"), "vis"),
        P(("row", "col"), "vis"),
    )
    out_specs = (
        P(("row", "col"), "vis"),
        P(("vis", "row", "col"), None),
        P("vis", ("row", "col")),
        P(("row", "col"), "vis"),
    )
    return jax.shard_map(
        on_device, mesh=mesh, in_specs=in_specs, out_specs=out_specs, check_vma=False
    )
```

profile of v0, /device:TPU:0, one launch (start us, length us, event | category | flops | bytes accessed | tf_op | source)
XLA Modules:
  0.0 442.7 jit_solution(14485268734717426963)
XLA Ops:
  7.2 1.1 convert_reduce_fusion
  8.3 1.0 fusion.33
  9.4 0.9 fusion.29
  10.3 0.1 all_to_all.30
  10.4 0.6 copy.18
  11.1 4.3 all-to-all-start
  15.3 0.9 select_reduce_fusion.5
  16.2 0.2 reduce-window.7
  16.4 0.1 convert_reduce_fusion.1
  16.5 0.7 select_reduce_fusion.3
  17.3 2.1 all-to-all-done
  19.4 32.0 %all_gather.6 = bf16[128,1600]{1,0:T(8,128)(2,1)S(1)} all-gather(bf16[16,1600]{1,0:T(8,128)(2,1)S(1)} %all_to_all.33), channel_id=1, replica_groups=mesh['vis'=4,'row'=4,'col'=2] {'row','col'}, dimensions={0}, use_global_device_ids=true | all-gather | bytes 460800 | tf_op jit(solution)/shard_map/all_gather | solution.py:95
  51.4 0.4 fusion.49
  51.8 0.7 gather_fusion
  52.5 0.7 select_convert_fusion
  53.2 0.0 all-reduce.9.cloned.1.call-start
  53.3 30.7 %all_gather.7 = bf16[64,1024]{1,0:T(8,128)(2,1)S(1)} all-gather(bf16[8,1024]{1,0:T(8,128)(2,1)} %param.21), channel_id=1, replica_groups=mesh['vis'=4,'row'=4,'col'=2] {'row','col'}, dimensions={0}, use_global_device_ids=true | all-gather | bytes 147456 | tf_op jit(solution)/shard_map/all_gather | solution.py:117
  84.0 1.0 all-reduce.7.cloned.1.call-done
  85.0 1.8 convolution_convert_fusion.5
  86.9 4.3 convolution_convert_fusion.1
  91.2 0.1 select_reduce_fusion.1
  91.3 68.2 %all-reduce.9.cloned.1.call-done = bf16[64,1024]{1,0:T(8,128)(2,1)} async-done(((bf16[64,1024]{1,0:T(8,128)(2,1)}), bf16[64,1024]{1,0:T(8,128)(2,1)}) %all-reduce.9.cloned.1.call-update) | async-done | bytes 131088 | tf_op jit(solution)/shard_map/psum | solution.py:100
  159.4 3.9 convolution_convert_fusion.2
  163.4 1.5 convolution_convert_fusion.3
  165.0 0.1 select_reduce_fusion.2
  165.1 34.1 %all-reduce.15.cloned.1.call-done = (bf16[64,2048]{1,0:T(8,128)(2,1)}, bf16[64,2048]{1,0:T(8,128)(2,1)}, bf16[64,2048]{1,0:T(8,128)(2,1)}) async-done(((bf16[64,2048]{1,0:T(8,128)(2,1)}, bf16[64,2048]{1,0:T(8,128)(2,1)}, bf16[64,2048]{1,0:T(8,128)(2,1)}), (bf16[64,2048]{1,0:T(8,128)(2,1)}, bf16[64,2048]{1,0:T(8,128)(2,1)}, bf16[64,2048]{1,0:T(8,128)(2,1)})) %all-reduce.15.cloned.1.call-update) | async-done | bytes 786448 | tf_op jit(solution)/shard_map/psum | solution.py:105
  199.3 4.0 fusion.13
  203.3 2.1 fusion
  205.4 70.6 %all-reduce.11.cloned.1.call-done = bf16[64,1024]{1,0:T(8,128)(2,1)} async-done(((bf16[64,1024]{1,0:T(8,128)(2,1)}), bf16[64,1024]{1,0:T(8,128)(2,1)}) %all-reduce.11.cloned.1.call-update) | async-done | bytes 131088 | tf_op jit(solution)/shard_map/psum | solution.py:124
  276.0 2.0 convolution_convert_fusion.6
  278.0 0.0 reduce-scatter.5.cloned.1.call-start
  278.0 31.3 %all-reduce.13.cloned.1.call-done = bf16[64,512]{1,0:T(8,128)(2,1)} async-done(((bf16[64,512]{1,0:T(8,128)(2,1)}), bf16[64,512]{1,0:T(8,128)(2,1)}) %all-reduce.13.cloned.1.call-update) | async-done | bytes 65552 | tf_op jit(solution)/shard_map/psum | solution.py:128
  309.4 0.9 fusion.23
  310.3 0.8 gather_fusion.1
  311.2 1.5 convolution_convert_fusion
  312.7 0.1 mul.268
  312.8 3.9 convolution_convert_fusion.4
  316.7 1.8 fusion.34
  318.5 2.4 fusion.48
  320.9 48.0 %reduce-scatter.5.cloned.1.call-done = bf16[16,1600]{1,0:T(8,128)(2,1)} async-done(((bf16[128,1600]{1,0:T(8,128)(2,1)}), bf16[16,1600]{1,0:T(8,128)(2,1)}) %reduce-scatter.5.cloned.1.call-update) | async-done | bytes 51216 | tf_op jit(solution)/shard_map/reduce_scatter | solution.py:134
  368.9 1.5 reshape.329
  370.4 3.3 all-to-all-start.1
  373.7 59.5 %reduce-scatter.3.cloned.1.call-done = bf16[8,1024]{1,0:T(8,128)(2,1)} async-done(((bf16[64,1024]{1,0:T(8,128)(2,1)}), bf16[8,1024]{1,0:T(8,128)(2,1)}) %reduce-scatter.3.cloned.1.call-update) | async-done | bytes 16400 | tf_op jit(solution)/shard_map/reduce_scatter | solution.py:109
  433.2 1.3 add_convert_fusion.3
  434.5 0.1 all_to_all.38
  434.7 0.2 fusion.30
  434.9 0.2 multiply_reduce_fusion
  435.1 0.8 fusion.32
  (54 shorter events, 0.5 us)
Async XLA Ops:
  7.2 44.2 %copy-start = (bf16[1600,512]{1,0:T(8,128)(2,1)S(1)}, bf16[1600,512]{1,0:T(8,128)(2,1)}, u32[]{:S(2)}) copy-start(bf16[1600,512]{1,0:T(8,128)(2,1)} %param.15) | copy-start | bytes 4915204
  7.2 77.8 %copy-start.3 = (bf16[512,1024]{1,0:T(8,128)(2,1)S(1)}, bf16[512,1024]{1,0:T(8,128)(2,1)}, u32[]{:S(2)}) copy-start(bf16[512,1024]{1,0:T(8,128)(2,1)} %param.17) | copy-start | bytes 3145732
  7.2 77.8 %copy-start.9 = (f32[512]{0:T(512)S(1)}, f32[512]{0:T(512)}, u32[]{:S(2)}) copy-start(f32[512]{0:T(512)} %param.16) | copy-start | bytes 6148
  11.1 8.3 %all-to-all-start = ((bf16[4,4,1600]{2,0,1:T(4,128)(2,1)}), bf16[4,4,1600]{2,0,1:T(4,128)(2,1)S(1)}, u32[]{:S(2)}, u32[]{:S(2)}) async-start(bf16[4,4,1600]{2,0,1:T(4,128)(2,1)} %copy.18), calls=%async_computation | async-start | bytes 106496 | tf_op jit(solution)/shard_map/all_to_all | solution.py:94
  15.3 69.7 %all-reduce.7.cloned.1.call-start = ((), (), s32[]{:S(2)}) async-start(), calls=%async_computation.4 | async-start | bytes 131072 | tf_op jit(solution)/shard_map/psum | solution.py:97
  51.4 39.8 %copy-start.10 = (s32[4]{0:T(128)S(1)}, s32[4]{0:T(128)}, u32[]{:S(2)}) copy-start(s32[4]{0:T(128)} %param.13) | copy-start | bytes 52
  53.2 106.2 %all-reduce.9.cloned.1.call-start = ((), (), s32[]{:S(2)}) async-start(), calls=%async_computation.5 | async-start | bytes 262144 | tf_op jit(solution)/shard_map/psum | solution.py:100
  86.8 112.4 %all-reduce.15.cloned.1.call-start = ((), (), s32[]{:S(2)}) async-start(), calls=%async_computation.10 | async-start | bytes 1572864 | tf_op jit(solution)/shard_map/psum | solution.py:105
  91.3 73.8 %copy-start.11 = (s32[4]{0:T(128)S(1)}, s32[4]{0:T(128)}, u32[]{:S(2)}) copy-start(s32[4]{0:T(128)} %param.12) | copy-start | bytes 52
  159.4 4.0 copy-start.1
  159.4 4.0 copy-start.5
  165.0 111.0 %all-reduce.11.cloned.1.call-start = ((), (), s32[]{:S(2)}) async-start(), calls=%async_computation.7 | async-start | bytes 262144 | tf_op jit(solution)/shard_map/psum | solution.py:124
  199.2 4.0 copy-start.2
  199.3 4.0 copy-start.12
  199.3 4.0 copy-start.13
  203.2 106.1 %copy-start.6 = (bf16[64,512]{1,0:T(8,128)(2,1)S(1)}, bf16[64,512]{1,0:T(8,128)(2,1)}, u32[]{:S(2)}) copy-start(bf16[64,512]{1,0:T(8,128)(2,1)} %all-reduce.7.cloned.1.call-done) | copy-start | bytes 196612
  205.3 107.4 %copy-start.8 = (f32[6400]{0:T(1024)S(1)}, f32[6400]{0:T(1024)}, u32[]{:S(2)}) copy-start(f32[6400]{0:T(1024)} %param.14) | copy-start | bytes 76804
  205.3 104.0 %all-reduce.13.cloned.1.call-start = ((), (), s32[]{:S(2)}) async-start(), calls=%async_computation.8 | async-start | bytes 131072 | tf_op jit(solution)/shard_map/psum | solution.py:128
  278.0 90.9 %reduce-scatter.5.cloned.1.call-start = ((), (), s32[]{:S(2)}) async-start(), calls=%async_computation.9 | async-start | bytes 479232 | tf_op jit(solution)/shard_map/reduce_scatter | solution.py:134
  311.1 5.5 %copy-start.7 = (bf16[64,1024]{1,0:T(8,128)(2,1)S(1)}, bf16[64,1024]{1,0:T(8,128)(2,1)}, u32[]{:S(2)}) copy-start(bf16[64,1024]{1,0:T(8,128)(2,1)} %all-reduce.11.cloned.1.call-done) | copy-start | bytes 393220
  312.6 120.5 %reduce-scatter.3.cloned.1.call-start = ((), (), s32[]{:S(2)}) async-start(), calls=%async_computation.6 | async-start | bytes 147456 | tf_op jit(solution)/shard_map/reduce_scatter | solution.py:109
  316.7 118.0 %copy-start.4 = (bf16[4,6400]{1,0:T(4,128)(2,1)S(1)}, bf16[4,6400]{1,0:T(4,128)(2,1)}, u32[]{:S(2)}) copy-start(bf16[4,6400]{1,0:T(4,128)(2,1)} %param.11) | copy-start | bytes 153604
  370.4 64.1 %all-to-all-start.1 = ((f32[4,4,1600]{2,1,0:T(4,128)}), f32[4,4,1600]{2,1,0:T(4,128)S(1)}, u32[]{:S(2)}, u32[]{:S(2)}) async-start(f32[4,4,1600]{2,1,0:T(4,128)} %reshape.329), calls=%async_computation.3 | async-start | bytes 212992 | tf_op jit(solution)/shard_map/all_to_all | solution.py:140
Sparse Core Ops, SparseCore 0:
  53.3 31.6 all-reduce.6
  88.9 70.4 all-reduce.8
  165.1 34.1 all-reduce.14
  205.5 70.4 all-reduce.10
  278.7 30.6 all-reduce.12
  312.8 56.1 reduce-scatter.4
  372.2 60.9 reduce-scatter.2
where the time goes:
time: 443 us
  waiting for transfers between devices  315 us (71%)
  blocking collectives  62.7 us (14%)
  matrix products  29.5 us (7%)
  between operations  14.3 us (3%)
  other arithmetic  9.34 us (2%)
  starting transfers between devices  7.82 us (2%)
    psum x1, waiting for transfers between devices, on_device(): lax.psum(input_part.astype(jnp.bfloat16), ('row', 'col'))  70.6 us
    psum x1, waiting for transfers between devices, on_device(): lax.psum(product(hidden_proj, proj_second).astype(jnp.bfloat16), ('row',...  68.2 us
    reduce_scatter x1, waiting for transfers between devices, on_device(): lax.psum_scatter(product(hidden, down_weight).astype(jnp.bfloat16), ('row...  59.5 us
    reduce_scatter x1, waiting for transfers between devices, on_device(): lax.psum_scatter(product(slot_act, proj_first.T).astype(jnp.bfloat16), ('...  48 us
    psum x1, waiting for transfers between devices, on_device(): lax.psum(up_part.astype(jnp.bfloat16), 'vis').astype(jnp.float32)  34.1 us
    all_gather x1, blocking collectives, on_device(): gathered = lax.all_gather(columns, ('row', 'col'), axis=0, tiled=True)  32 us
    psum x1, waiting for transfers between devices, on_device(): lax.psum(pre_part.astype(jnp.bfloat16), 'vis').astype(jnp.float32)  31.3 us
    all_gather x1, blocking collectives, on_device(): upstream = lax.all_gather(cotangent, ('row', 'col'), axis=0, tiled=True)  30.7 us
  transfers between devices with their start and end apart: 9, of which 8 were waited for; matrix products, arithmetic and copies ran while one was open for 4% of the time, Pallas kernels for 0%

commit v1 on v0

v1 whole, which is shorter than its diff:
```python
import functools

import jax
import jax.numpy as jnp
from jax import lax
from jax.experimental import pallas as pl
from jax.experimental.pallas import tpu as pltpu
from jax.sharding import PartitionSpec as P


def row_tables(counts, block_order, total_rows, per_device, group_size):
    vision = counts.shape[0]
    labels = jnp.arange(vision, dtype=jnp.int32)
    chosen = (block_order[:, None] == labels[None, :]).astype(jnp.int32)
    ordered = jnp.sum(chosen * counts[None, :], axis=1)
    block_ends = jnp.cumsum(ordered)
    block_starts = block_ends - ordered
    language = jnp.arange(total_rows, dtype=jnp.int32)
    block_of = jnp.sum((block_ends[None, :] <= language[:, None]).astype(jnp.int32), axis=1)
    picked = (block_of[:, None] == labels[None, :]).astype(jnp.int32)
    owner = jnp.sum(picked * block_order[None, :], axis=1)
    offset = language - jnp.sum(picked * block_starts[None, :], axis=1)
    stride = vision * per_device
    source = offset // per_device * stride + owner * per_device + offset % per_device
    slots = jnp.arange(stride * group_size, dtype=jnp.int32)
    within = slots % stride
    slot_owner = within // per_device
    slot_offset = slots // stride * per_device + within % per_device
    owner_start = jnp.sum(chosen * block_starts[:, None], axis=0)
    matched = (slot_owner[:, None] == labels[None, :]).astype(jnp.int32)
    start_of = jnp.sum(matched * owner_start[None, :], axis=1)
    count_of = jnp.sum(matched * counts[None, :], axis=1)
    live = slot_offset < count_of
    target = jnp.where(live, start_of + slot_offset, 0)
    return (source, target, live)


def gelu_parts(pre):
    normal_cdf = 0.5 * (1.0 + jax.scipy.special.erf(pre * 0.7071067811865476))
    density = jnp.exp(-0.5 * pre * pre) * 0.3989422804014327
    return (pre * normal_cdf, normal_cdf + pre * density)


def apply_layer_norm(images, projector_norm_gain):
    values = images.astype(jnp.float32)
    mean_removed = values - jnp.mean(values, axis=-1, keepdims=True)
    variance = jnp.mean(mean_removed * mean_removed, axis=-1, keepdims=True)
    inverse_scale = lax.rsqrt(variance + 1e-05)
    standardized_input = mean_removed * inverse_scale
    return (
        standardized_input,
        inverse_scale,
        (standardized_input * projector_norm_gain).astype(jnp.bfloat16),
    )


def norm_gradient_pass(gradient_tuple, standardized_input, inverse_scale, projector_norm_gain):
    gain_scaled = gradient_tuple * projector_norm_gain
    return inverse_scale * (
        gain_scaled
        - jnp.mean(gain_scaled, axis=-1, keepdims=True)
        - standardized_input * jnp.mean(gain_scaled * standardized_input, axis=-1, keepdims=True)
    )


def product(left, right):
    return jnp.dot(left, right, preferred_element_type=jnp.float32)


def feed_grads(hidden_grad, gate_sum, up_sum, gate_sigmoid):
    gate_grad = (
        hidden_grad * up_sum * gate_sigmoid * (1.0 + gate_sum * (1.0 - gate_sigmoid))
    ).astype(jnp.bfloat16)
    up_grad = (hidden_grad * gate_sum * gate_sigmoid).astype(jnp.bfloat16)
    return (gate_grad, up_grad)


MESH = pl.DeviceIdType.MESH
BF = jnp.bfloat16
F32 = jnp.float32
ANY = pl.BlockSpec(memory_space=pl.ANY)
VM = pl.BlockSpec(memory_space=pltpu.VMEM)
TILES = 4


def dot_nt(left, right):
    return lax.dot_general(left, right, (((1,), (1,)), ((), ())), preferred_element_type=F32)


def entry_barrier(n, me, coords):
    barrier = pltpu.get_barrier_semaphore()

    def signal(k, carry):
        pl.semaphore_signal(
            barrier, inc=1, device_id=coords(lax.rem(me + k, n)), device_id_type=MESH
        )
        return carry

    lax.fori_loop(1, n, signal, 0)
    return barrier


def spread(src_of, dst, n, me, coords, send_sem, recv_sem):
    def body(k, carry):
        p = lax.rem(me + k, n)
        pltpu.make_async_remote_copy(
            src_ref=src_of(p),
            dst_ref=dst.at[me],
            send_sem=send_sem,
            recv_sem=recv_sem,
            device_id=coords(p),
            device_id_type=MESH,
        ).start()
        return carry

    lax.fori_loop(1, n, body, 0)


def wait_for(buf, n, sem):
    view = buf.at[pl.ds(0, n - 1)]
    pltpu.make_async_copy(view, view, sem).wait()


def flat_coords(sizes, p):
    n_vis, _, n_col = sizes
    return (p % n_vis, p // n_vis // n_col, p // n_vis % n_col)


def my_place(sizes):
    n_vis, _, n_col = sizes
    vis, row, col = lax.axis_index("vis"), lax.axis_index("row"), lax.axis_index("col")
    return vis, row, col, (row * n_col + col) * n_vis + vis


def gather_kernel(sizes, blocks, cot, rows_out, cot_out, sems):
    n_vis, n_row, n_col = sizes
    group = n_row * n_col
    n_dev = n_vis * group
    vis, row, col, me = my_place(sizes)
    pos = row * n_col + col
    barrier = entry_barrier(n_dev, me, lambda p: flat_coords(sizes, p))
    pl.semaphore_wait(barrier, n_dev - 1)
    spread(
        lambda p: blocks.at[lax.rem(p, n_vis)], rows_out, n_dev, me,
        lambda p: flat_coords(sizes, p), sems.at[0], sems.at[1],
    )
    spread(
        lambda p: cot, cot_out, group, pos,
        lambda p: (vis, p // n_col, p % n_col), sems.at[2], sems.at[3],
    )
    rows_out[me] = blocks[vis]
    cot_out[pos] = cot[...]
    wait_for(rows_out, n_dev, sems.at[1])
    wait_for(cot_out, group, sems.at[3])
    wait_for(rows_out, n_dev, sems.at[0])
    wait_for(cot_out, group, sems.at[2])


def return_kernel(sizes, slabs, recv, sems):
    n_vis, n_row, n_col = sizes
    n_dev = n_vis * n_row * n_col
    _, _, _, me = my_place(sizes)
    barrier = entry_barrier(n_dev, me, lambda p: flat_coords(sizes, p))
    pl.semaphore_wait(barrier, n_dev - 1)
    spread(
        lambda p: slabs.at[p], recv, n_dev, me,
        lambda p: flat_coords(sizes, p), sems.at[0], sems.at[1],
    )
    recv[me] = slabs[me]
    wait_for(recv, n_dev, sems.at[1])
    wait_for(recv, n_dev, sems.at[0])


def middle_kernel(
    sizes, packed, upstream, bias, wf_hbm, ws_hbm, wg_hbm, wu_hbm, wd_hbm,
    block_out, act_out, hid_out, ig_out,
    wf, ws, wg, wu, wd,
    b_part, b_recv, b_all, h_part, h_recv, h_all, c_part, c_recv, c_all,
    d_part, d_recv, d_all, e_part, e_recv, e_all, o_part, o_recv, f_part, f_recv, f_all,
    slope, inputs, acc, hidden, wsem, sems,
):
    n_vis, n_row, n_col = sizes
    group = n_row * n_col
    vis, row, col, _ = my_place(sizes)
    pos = row * n_col + col
    rows = packed.shape[0]
    vr, gr = rows // n_vis, rows // group
    ffl = wg.shape[1]
    tw = ffl // TILES

    def in_vis(p):
        return (p, row, col)

    def in_group(p):
        return (vis, p // n_col, p % n_col)

    loads = {}
    for i, (name, src, dst) in enumerate(
        (("wf", wf_hbm, wf), ("wd", wd_hbm, wd), ("ws", ws_hbm, ws), ("wg", wg_hbm, wg), ("wu", wu_hbm, wu))
    ):
        loads[name] = pltpu.make_async_copy(src, dst, wsem.at[i])
        loads[name].start()
    barrier = entry_barrier(n_vis, vis, in_vis)
    entry_barrier(group, pos, in_group)

    used = []

    def start(idx, src_of, dst, n, me, coords):
        spread(src_of, dst, n, me, coords, sems.at[2 * idx], sems.at[2 * idx + 1])
        used.append((idx, dst, n))

    def arrive(idx, dst, n):
        wait_for(dst, n, sems.at[2 * idx + 1])

    def fill(part, value, n, chunk):
        for i in range(n):
            part[i] = value[i * chunk:(i + 1) * chunk].astype(BF)

    def total(recv, part, n, me):
        recv[me] = part[me]
        result = recv[0].astype(F32)
        for i in range(1, n):
            result = result + recv[i].astype(F32)
        return result

    def whole(buf, n):
        return jnp.concatenate([buf[i].astype(F32) for i in range(n)], axis=0)

    loads["wf"].wait()
    fill(b_part, jnp.dot(packed[...], wf[...], preferred_element_type=F32), n_vis, vr)
    pl.semaphore_wait(barrier, n_vis - 1 + group - 1)
    start(0, lambda p: b_part.at[p], b_recv, n_vis, vis, in_vis)

    loads["wd"].wait()
    for t in range(TILES):
        cols = slice(t * tw, (t + 1) * tw)
        value = dot_nt(upstream[...], wd[cols, :])
        for i in range(n_vis):
            h_part[i, :, cols] = value[i * vr:(i + 1) * vr].astype(BF)

    arrive(0, b_recv, n_vis)
    b_all[vis] = total(b_recv, b_part, n_vis, vis).astype(BF)
    start(1, lambda p: b_all.at[vis], b_all, n_vis, vis, in_vis)
    start(2, lambda p: h_part.at[p], h_recv, n_vis, vis, in_vis)
    arrive(1, b_all, n_vis)
    pre = whole(b_all, n_vis) + bias[...]
    activated, slope_value = gelu_parts(pre)
    slope[...] = slope_value
    hid_out[...] = activated.astype(BF)

    loads["ws"].wait()
    fill(c_part, jnp.dot(hid_out[...], ws[...], preferred_element_type=F32), group, gr)
    start(3, lambda p: c_part.at[p], c_recv, group, pos, in_group)
    arrive(2, h_recv, n_vis)
    h_all[vis] = total(h_recv, h_part, n_vis, vis).astype(BF)
    start(4, lambda p: h_all.at[vis], h_all, n_vis, vis, in_vis)
    arrive(3, c_recv, group)
    c_all[pos] = total(c_recv, c_part, group, pos).astype(BF)
    start(5, lambda p: c_all.at[pos], c_all, group, pos, in_group)
    arrive(5, c_all, group)
    inputs[...] = whole(c_all, group).astype(BF)

    loads["wg"].wait()
    loads["wu"].wait()
    arrive(4, h_all, n_vis)
    for t in range(TILES):
        cols = slice(t * tw, (t + 1) * tw)
        for half, weight in enumerate((wg, wu)):
            value = jnp.dot(inputs[...], weight[:, cols], preferred_element_type=F32)
            for i in range(n_vis):
                d_part[t, i, :, half * tw:(half + 1) * tw] = value[i * vr:(i + 1) * vr].astype(BF)
        start(6 + t, lambda p, t=t: d_part.at[t, p], d_recv.at[t], n_vis, vis, in_vis)
    for t in range(TILES):
        arrive(6 + t, d_recv.at[t], n_vis)
        d_all[t, vis] = total(d_recv.at[t], d_part.at[t], n_vis, vis).astype(BF)
        start(6 + TILES + t, lambda p, t=t: d_all.at[t, vis], d_all.at[t], n_vis, vis, in_vis)
    for t in range(TILES):
        cols = slice(t * tw, (t + 1) * tw)
        arrive(6 + TILES + t, d_all.at[t], n_vis)
        both = whole(d_all.at[t], n_vis)
        gate_sum, up_sum = both[:, :tw], both[:, tw:]
        hidden_grad = jnp.concatenate([h_all[i, :, cols].astype(F32) for i in range(n_vis)], axis=0)
        gate_sigmoid = jax.nn.sigmoid(gate_sum)
        hidden[:, cols] = (gate_sum * gate_sigmoid * up_sum).astype(BF)
        gate_grad, up_grad = feed_grads(hidden_grad, gate_sum, up_sum, gate_sigmoid)
        value = dot_nt(gate_grad, wg[:, cols]) + dot_nt(up_grad, wu[:, cols])
        if t == 0:
            acc[...] = value
        else:
            acc[...] += value
    base = 6 + 2 * TILES
    fill(e_part, acc[...], group, gr)
    start(base, lambda p: e_part.at[p], e_recv, group, pos, in_group)

    fill(o_part, jnp.dot(hidden[...], wd[...], preferred_element_type=F32), group, gr)
    arrive(base, e_recv, group)
    mine = pl.ds(pl.multiple_of(pos * gr, gr), gr)
    e_all[pos] = (total(e_recv, e_part, group, pos) + upstream[mine, :].astype(F32)).astype(BF)
    start(base + 1, lambda p: e_all.at[pos], e_all, group, pos, in_group)
    start(base + 2, lambda p: o_part.at[p], o_recv, group, pos, in_group)
    arrive(base + 1, e_all, group)
    ig_out[...] = whole(e_all, group).astype(BF)
    fill(f_part, dot_nt(ig_out[...], ws[...]), n_vis, vr)
    start(base + 3, lambda p: f_part.at[p], f_recv, n_vis, vis, in_vis)
    arrive(base + 3, f_recv, n_vis)
    f_all[vis] = total(f_recv, f_part, n_vis, vis).astype(BF)
    start(base + 4, lambda p: f_all.at[vis], f_all, n_vis, vis, in_vis)
    arrive(base + 2, o_recv, group)
    block_out[...] = (c_all[pos].astype(F32) + total(o_recv, o_part, group, pos)).astype(BF)
    arrive(base + 4, f_all, n_vis)
    act_out[...] = (whole(f_all, n_vis) * slope[...]).astype(BF)
    for idx, dst, n in used:
        wait_for(dst, n, sems.at[2 * idx])


def slabs_of(n, *shape):
    return [pltpu.VMEM((n,) + shape, BF)] * 3


def on_device(
    sizes,
    images,
    counts,
    block_order,
    projector_norm_gain,
    proj_first,
    proj_bias,
    proj_second,
    gate_weight,
    up_weight,
    down_weight,
    cotangent,
):
    n_vis, n_row, n_col = sizes
    group_size = n_row * n_col
    n_dev = n_vis * group_size
    per_device = images.shape[0]
    local_rows = cotangent.shape[0]
    rows = local_rows * group_size
    vf, pl_units = proj_first.shape
    dl, ffl = gate_weight.shape
    source, target, live = row_tables(counts, block_order, rows, per_device, group_size)
    standardized_input, inverse_scale, norm_output = apply_layer_norm(images, projector_norm_gain)
    blocks = jnp.swapaxes(norm_output.reshape(per_device, n_vis, vf), 0, 1)
    gathered, upstream = pl.pallas_call(
        functools.partial(gather_kernel, sizes),
        out_shape=(
            jax.ShapeDtypeStruct((n_dev, per_device, vf), BF),
            jax.ShapeDtypeStruct((group_size, local_rows, dl), BF),
        ),
        in_specs=[VM, VM],
        out_specs=(VM, VM),
        scratch_shapes=[pltpu.SemaphoreType.DMA((4,))],
        compiler_params=pltpu.CompilerParams(collective_id=0, has_side_effects=True),
    )(blocks, cotangent)
    upstream = upstream.reshape(rows, dl)
    packed = jnp.take(gathered.reshape(n_dev * per_device, vf), source, axis=0)
    vr = rows // n_vis
    n_sems = 2 * (6 + 2 * TILES + 5)
    block_out, act_grad, hidden_proj, input_grad = pl.pallas_call(
        functools.partial(middle_kernel, sizes),
        out_shape=(
            jax.ShapeDtypeStruct((local_rows, dl), BF),
            jax.ShapeDtypeStruct((rows, pl_units), BF),
            jax.ShapeDtypeStruct((rows, pl_units), BF),
            jax.ShapeDtypeStruct((rows, dl), BF),
        ),
        in_specs=[VM, VM, VM, ANY, ANY, ANY, ANY, ANY],
        out_specs=(VM, VM, VM, VM),
        scratch_shapes=[
            pltpu.VMEM(proj_first.shape, BF),
            pltpu.VMEM(proj_second.shape, BF),
            pltpu.VMEM(gate_weight.shape, BF),
            pltpu.VMEM(up_weight.shape, BF),
            pltpu.VMEM(down_weight.shape, BF),
            *slabs_of(n_vis, vr, pl_units),
            *slabs_of(n_vis, vr, ffl),
            *slabs_of(group_size, local_rows, dl),
            *slabs_of(TILES, n_vis, vr, 2 * ffl // TILES),
            *slabs_of(group_size, local_rows, dl),
            *slabs_of(group_size, local_rows, dl)[:2],
            *slabs_of(n_vis, vr, pl_units),
            pltpu.VMEM((rows, pl_units), F32),
            pltpu.VMEM((rows, dl), BF),
            pltpu.VMEM((rows, dl), F32),
            pltpu.VMEM((rows, ffl), BF),
            pltpu.SemaphoreType.DMA((5,)),
            pltpu.SemaphoreType.DMA((n_sems,)),
        ],
        compiler_params=pltpu.CompilerParams(
            collective_id=1, has_side_effects=True, vmem_limit_bytes=48 << 20
        ),
    )(
        packed, upstream, proj_bias[None, :], proj_first, proj_second,
        gate_weight, up_weight, down_weight,
    )
    slot_act = jnp.where(
        live[:, None], jnp.take(act_grad, target, axis=0), jnp.zeros((), BF)
    )
    slot_part = dot_nt(slot_act, proj_first).astype(BF)
    returned = pl.pallas_call(
        functools.partial(return_kernel, sizes),
        out_shape=jax.ShapeDtypeStruct((n_dev, per_device, vf), BF),
        in_specs=[VM],
        out_specs=VM,
        scratch_shapes=[pltpu.SemaphoreType.DMA((2,))],
        compiler_params=pltpu.CompilerParams(collective_id=2, has_side_effects=True),
    )(slot_part.reshape(n_dev, per_device, vf))
    returned = jnp.sum(returned.reshape(group_size, n_vis, per_device, vf).astype(F32), axis=0)
    image_slot_gradients = norm_gradient_pass(
        jnp.swapaxes(returned, 0, 1).reshape(per_device, n_vis * vf),
        standardized_input, inverse_scale, projector_norm_gain,
    )
    second_grad = product(hidden_proj.T, input_grad)
    first_grad = product(packed.T, act_grad)
    return (block_out, image_slot_gradients, first_grad, second_grad)


def solution(mesh):
    in_specs = (
        P(("vis", "row", "col"), None),
        P(),
        P(),
        P(),
        P("vis", ("row", "col")),
        P(("row", "col")),
        P(("row", "col"), "vis"),
        P("vis", ("row", "col")),
        P("vis", ("row", "col")),
        P(("row", "col"), "vis"),
        P(("row", "col"), "vis"),
    )
    out_specs = (
        P(("row", "col"), "vis"),
        P(("vis", "row", "col"), None),
        P("vis", ("row", "col")),
        P(("row", "col"), "vis"),
    )
    sizes = (mesh.shape["vis"], mesh.shape["row"], mesh.shape["col"])
    return jax.shard_map(
        functools.partial(on_device, sizes), mesh=mesh, in_specs=in_specs, out_specs=out_specs, check_vma=False
    )
```

time: 443 us -> 105 us (0.24)
  waiting for transfers between devices: 315 us -> 0 us
  Pallas kernels: 0 us -> 84.8 us
  blocking collectives: 62.7 us -> 0 us
  matrix products: 29.5 us -> 4.76 us
  between operations: 14.3 us -> 0.85 us
  starting transfers between devices: 7.82 us -> 0 us
    psum x5 -> x0, waiting for transfers between devices: 205 us -> none  [the longest x1 70.6 us: on_device(): lax.psum(input_part.astype(jnp.bfloat16), ('row', 'col'))]
    reduce_scatter x2 -> x0, waiting for transfers between devices: 108 us -> none  [the longest x1 59.5 us: on_device(): lax.psum_scatter(product(hidden, down_weight).astype(jnp.bfloat16), ('row...]
    pallas_call x0 -> x3, Pallas kernels: none -> 84.8 us  [the longest x1 48.7 us: on_device(): pl.pallas_call(functools.partial(middle_kernel, sizes), out_shape=(jax.Sh...]
    all_gather x2 -> x0, blocking collectives: 62.7 us -> none  [the longest x1 32 us: on_device(): gathered = lax.all_gather(columns, ('row', 'col'), axis=0, tiled=True)]
    dot_general x12 -> x2, matrix products: 29.5 us -> 4.09 us  [product(): return jnp.dot(left, right, preferred_element_type=jnp.float32)]
    all_to_all x2 -> x0, starting transfers between devices: 7.57 us -> none  [the longest x1 4.26 us: on_device(): lax.all_to_all(norm_output, 'vis', split_axis=1, concat_axis=0, tiled=True)]
  transfers between devices with their start and end apart: 9 -> 0, of which waited for: 8 -> 0; matrix products, arithmetic and copies ran while one was open for 4% -> 0% of each run, Pallas kernels for 0% -> 0%
where the time goes in v1:
time: 105 us; the launch traced here: 104 us
  Pallas kernels  84.8 us (81%)
  other arithmetic  7.71 us (7%)
  local copies, waits for them, and re-layouts  5.64 us (5%)
  matrix products  4.76 us (5%)
    pallas_call x1, Pallas kernels, on_device(): pl.pallas_call(functools.partial(middle_kernel, sizes), out_shape=(jax.Sh...  48.7 us
    pallas_call x1, Pallas kernels, on_device(): pl.pallas_call(functools.partial(gather_kernel, sizes), out_shape=(jax.Sh...  21.6 us
    pallas_call x1, Pallas kernels, on_device(): pl.pallas_call(functools.partial(return_kernel, sizes), out_shape=jax.Sha...  14.4 us
    dot_general x2, matrix products, product(): return jnp.dot(left, right, preferred_element_type=jnp.float32)  4.09 us

profile of v1, /device:TPU:0, one launch (start us, length us, event | category | flops | bytes accessed | tf_op | source)
XLA Modules:
  0.0 103.7 jit_solution(14872061196770350823)
XLA Ops:
  0.6 0.0 copy-start.3
  0.6 0.0 copy-start
  0.7 0.0 copy-start.1
  0.7 1.1 %convert_reduce_fusion.1 = f32[4]{0:T(128)S(1)} fusion(bf16[4,6400]{1,0:T(4,128)(2,1)} %param.11), kind=kLoop, calls=%fused_computation.10 | loop fusion | flops 51196 | bytes 51216 | tf_op jit(solution)/shard_map/reduce_sum | solution.py:46
  1.8 1.0 %fusion.13 = f32[4]{0:T(128)S(1)} fusion(bf16[4,6400]{1,0:T(4,128)(2,1)} %param.11, f32[4]{0:T(128)S(1)} %broadcast_multiply_fusion.2), kind=kLoop, calls=%fused_computation.21 | loop fusion | flops 102396 | bytes 51232 | tf_op jit(solution)/shard_map/reduce_sum | solution.py:47
  2.8 0.9 fusion.9
  3.8 0.1 reshape.339
  3.9 0.6 copy.27
  4.5 21.6 %shard_map.138 = (bf16[32,4,1600]{2,1,0:T(4,128)(2,1)}, bf16[8,8,1024]{2,1,0:T(8,128)(2,1)}) custom-call(bf16[4,4,1600]{2,1,0:T(4,128)(2,1)} %bitcast.47, bf16[8,1024]{1,0:T(8,128)(2,1)} %cot.1), custom_call_target="tpu_custom_call" | custom-call | tf_op jit(solution)/shard_map/pallas_call | solution.py:345
  26.2 0.0 copy-start.2
  26.2 1.2 %reshape.340 = bf16[128,1600]{1,0:T(8,128)(2,1)S(1)} reshape(bf16[32,4,1600]{2,1,0:T(4,128)(2,1)} %get-tuple-element.10) | data formatting | bytes 819200 | tf_op jit(solution)/shard_map/reshape | solution.py:357
  27.4 0.9 select_reduce_fusion.5
  28.3 0.2 reduce-window.7
  28.5 0.1 convert_reduce_fusion.2
  28.5 0.7 select_reduce_fusion.3
  29.3 0.8 gather_fusion
  30.1 0.1 broadcast_select_fusion.packed
  30.2 0.0 copy-done.3
  30.2 0.0 copy-done
  30.2 0.0 copy-done.1
  30.2 0.0 copy-done.2
  30.2 0.0 copy-start.6
  30.2 0.0 copy-start.7
  30.3 48.7 %shard_map.139 = (bf16[8,1024]{1,0:T(8,128)(2,1)S(1)}, bf16[64,512]{1,0:T(8,128)(2,1)S(1)}, bf16[64,512]{1,0:T(8,128)(2,1)S(1)}, bf16[64,1024]{1,0:T(8,128)(2,1)S(1)}) custom-call(bf16[64,1600]{1,0:T(8,128)(2,1)S(1)} %broadcast_select_fusion.packed, bf16[64,1024]{1,0:T(8,128)(2,1)S(1)} %bitcast.43, f32[1,512]{1,0:T(1,128)S(1)} %bitcast.44, ...), custom_call_target="tpu_custom_call" | custom-call | tf_op jit(solution)/shard_map/pallas_call | solution.py:360
  79.0 0.0 copy-done.6
  79.0 0.1 select_reduce_fusion.1
  79.1 0.0 copy-done.7
  79.1 0.1 select_reduce_fusion.2
  79.2 0.8 gather_fusion.1
  80.1 0.7 convolution_convert_fusion
  80.7 0.0 copy-start.4
  80.8 0.0 copy-start.5
  80.8 0.3 copy.24
  81.0 0.9 reshape.342.slabs
  81.9 14.4 %shard_map.140 = bf16[32,4,1600]{2,1,0:T(4,128)(2,1)} custom-call(bf16[32,4,1600]{2,1,0:T(4,128)(2,1)} %reshape.342.slabs), custom_call_target="tpu_custom_call" | custom-call | tf_op jit(solution)/shard_map/pallas_call | solution.py:401
  96.3 1.2 %convert_reduce_fusion = f32[4,4,1600]{2,1,0:T(4,128)S(1)} fusion(bf16[8,4,4,1600]{3,2,1,0:T(4,128)(2,1)} %bitcast.45), kind=kLoop, calls=%fused_computation.3 | loop fusion | flops 384000 | bytes 512000 | tf_op jit(solution)/shard_map/reduce_sum | solution.py:409
  97.6 0.1 reshape.343
  97.7 0.0 copy-done.4
  97.7 0.0 copy-done.5
  97.8 0.2 fusion.10
  98.0 0.1 mul.180
  98.1 0.2 multiply_reduce_fusion
  98.3 0.8 fusion.12
  99.0 2.3 %fusion.28 = f32[1600,512]{1,0:T(8,128)} fusion(bf16[64,1600]{1,0:T(8,128)(2,1)S(1)} %broadcast_select_fusion.packed, bf16[64,512]{1,0:T(8,128)(2,1)S(1)} %get-tuple-element.13), kind=kOutput, calls=%fused_computation.93 | convolution fusion | flops 104857600 | bytes 3547136 | tf_op jit(solution)/shard_map/dot_general | solution.py:67
  101.3 1.8 %fusion.29 = f32[512,1024]{1,0:T(8,128)} fusion(bf16[64,512]{1,0:T(8,128)(2,1)S(1)} %get-tuple-element.14, bf16[64,1024]{1,0:T(8,128)(2,1)S(1)} %get-tuple-element.15), kind=kOutput, calls=%fused_computation.94 | convolution fusion | flops 67108864 | bytes 2293760 | tf_op jit(solution)/shard_map/dot_general | solution.py:67
  103.1 0.6 copy.29
  (12 shorter events, 0.1 us)
Async XLA Ops:
  0.6 29.6 %copy-start.3 = (f32[512]{0:T(512)S(1)}, f32[512]{0:T(512)}, u32[]{:S(2)}) copy-start(f32[512]{0:T(512)} %param.16) | copy-start | bytes 6148
  0.6 29.6 %copy-start = (bf16[1600,512]{1,0:T(8,128)(2,1)S(1)}, bf16[1600,512]{1,0:T(8,128)(2,1)}, u32[]{:S(2)}) copy-start(bf16[1600,512]{1,0:T(8,128)(2,1)} %wf_hbm.1) | copy-start | bytes 4915204
  0.7 29.6 %copy-start.1 = (bf16[512,1024]{1,0:T(8,128)(2,1)S(1)}, bf16[512,1024]{1,0:T(8,128)(2,1)}, u32[]{:S(2)}) copy-start(bf16[512,1024]{1,0:T(8,128)(2,1)} %ws_hbm.1) | copy-start | bytes 3145732
  26.2 4.1 %copy-start.2 = (bf16[8,8,1024]{2,1,0:T(8,128)(2,1)S(1)}, bf16[8,8,1024]{2,1,0:T(8,128)(2,1)}, u32[]{:S(2)}) copy-start(bf16[8,8,1024]{2,1,0:T(8,128)(2,1)} %get-tuple-element.11) | copy-start | bytes 393220
  30.2 48.8 %copy-start.6 = (s32[4]{0:T(128)S(1)}, s32[4]{0:T(128)}, u32[]{:S(2)}) copy-start(s32[4]{0:T(128)} %param.13) | copy-start | bytes 52
  30.2 48.8 %copy-start.7 = (s32[4]{0:T(128)S(1)}, s32[4]{0:T(128)}, u32[]{:S(2)}) copy-start(s32[4]{0:T(128)} %param.12) | copy-start | bytes 52
  80.7 17.0 %copy-start.4 = (bf16[4,6400]{1,0:T(4,128)(2,1)S(1)}, bf16[4,6400]{1,0:T(4,128)(2,1)}, u32[]{:S(2)}) copy-start(bf16[4,6400]{1,0:T(4,128)(2,1)} %param.11) | copy-start | bytes 153604
  80.8 17.0 %copy-start.5 = (f32[6400]{0:T(1024)S(1)}, f32[6400]{0:T(1024)}, u32[]{:S(2)}) copy-start(f32[6400]{0:T(1024)} %param.14) | copy-start | bytes 76804

commit v2 on v1

v2 whole, which is shorter than its diff:
```python
import functools

import jax
import jax.numpy as jnp
from jax import lax
from jax.experimental import pallas as pl
from jax.experimental.pallas import tpu as pltpu
from jax.sharding import PartitionSpec as P


def gelu_parts(pre):
    normal_cdf = 0.5 * (1.0 + jax.scipy.special.erf(pre * 0.7071067811865476))
    density = jnp.exp(-0.5 * pre * pre) * 0.3989422804014327
    return (pre * normal_cdf, normal_cdf + pre * density)


def norm_gradient_pass(gradient_tuple, standardized_input, inverse_scale, projector_norm_gain):
    gain_scaled = gradient_tuple * projector_norm_gain
    return inverse_scale * (
        gain_scaled
        - jnp.mean(gain_scaled, axis=-1, keepdims=True)
        - standardized_input * jnp.mean(gain_scaled * standardized_input, axis=-1, keepdims=True)
    )


def product(left, right):
    return jnp.dot(left, right, preferred_element_type=jnp.float32)


def feed_grads(hidden_grad, gate_sum, up_sum, gate_sigmoid):
    gate_grad = (
        hidden_grad * up_sum * gate_sigmoid * (1.0 + gate_sum * (1.0 - gate_sigmoid))
    ).astype(jnp.bfloat16)
    up_grad = (hidden_grad * gate_sum * gate_sigmoid).astype(jnp.bfloat16)
    return (gate_grad, up_grad)


MESH = pl.DeviceIdType.MESH
BF = jnp.bfloat16
F32 = jnp.float32
ANY = pl.BlockSpec(memory_space=pl.ANY)
VM = pl.BlockSpec(memory_space=pltpu.VMEM)
TILES = 4


def dot_nt(left, right):
    return lax.dot_general(left, right, (((1,), (1,)), ((), ())), preferred_element_type=F32)


def entry_barrier(n, me, coords):
    barrier = pltpu.get_barrier_semaphore()

    def signal(k, carry):
        pl.semaphore_signal(
            barrier, inc=1, device_id=coords(lax.rem(me + k, n)), device_id_type=MESH
        )
        return carry

    lax.fori_loop(1, n, signal, 0)
    return barrier


def spread(src_of, dst, n, me, coords, send_sem, recv_sem):
    def body(k, carry):
        p = lax.rem(me + k, n)
        pltpu.make_async_remote_copy(
            src_ref=src_of(p),
            dst_ref=dst.at[me],
            send_sem=send_sem,
            recv_sem=recv_sem,
            device_id=coords(p),
            device_id_type=MESH,
        ).start()
        return carry

    lax.fori_loop(1, n, body, 0)


def wait_for(view, sem):
    pltpu.make_async_copy(view, view, sem).wait()


def flat_coords(sizes, p):
    n_vis, _, n_col = sizes
    return (p % n_vis, p // n_vis // n_col, p // n_vis % n_col)


def my_place(sizes):
    n_vis, _, n_col = sizes
    vis, row, col = lax.axis_index("vis"), lax.axis_index("row"), lax.axis_index("col")
    return vis, row, col, (row * n_col + col) * n_vis + vis


def row_places(counts, order, n_vis, per, shape, axis):
    slots = lax.broadcasted_iota(jnp.int32, shape, axis)
    owner = slots // per % n_vis
    offset = slots // (n_vis * per) * per + slots % per
    start_of = jnp.zeros(shape, jnp.int32)
    count_of = jnp.zeros(shape, jnp.int32)
    begin = jnp.int32(0)
    for b in range(n_vis):
        device = order[b]
        live_rows = counts[device]
        start_of = jnp.where(owner == device, begin, start_of)
        count_of = jnp.where(owner == device, live_rows, count_of)
        begin = begin + live_rows
    return jnp.where(offset < count_of, start_of + offset, -1)


def chain_kernel(
    sizes, counts, order, images, gain, cot, bias, wf_hbm, ws_hbm, wg_hbm, wu_hbm, wd_hbm,
    block_out, slot_out, packed_out, act_out, hid_out, ig_out,
    wf, ws, wg, wu, wd,
    blocks, rows_all, cot_all, upstream, slabs, slabs_recv,
    b_part, b_pair, b_ring, b_all, h_part, h_pair, h_ring, h_all,
    d_part, d_pair, d_ring, d_all, f_part, f_pair, f_ring, f_all,
    c_part, c_recv, c_all, e_part, e_recv, e_all, o_part, o_recv,
    slope, inputs, acc, hidden, wsem, sems,
):
    n_vis, n_row, n_col = sizes
    group = n_row * n_col
    n_dev = n_vis * group
    vis, row, col, me = my_place(sizes)
    pos = row * n_col + col
    core, ring_at, n_ring = lax.rem(vis, 2), vis // 2, n_vis // 2
    per, vf = blocks.shape[1:]
    rows, dl = upstream.shape
    gr, hr = rows // group, rows // 2
    ffl = wg.shape[1]
    tw = ffl // TILES

    def everyone(p):
        return flat_coords(sizes, p)

    def in_ring(p):
        return (2 * p + core, row, col)

    def in_group(p):
        return (vis, p // n_col, p % n_col)

    loads = {}
    for i, (name, src, dst) in enumerate(
        (("wd", wd_hbm, wd), ("wf", wf_hbm, wf), ("ws", ws_hbm, ws), ("wg", wg_hbm, wg), ("wu", wu_hbm, wu))
    ):
        loads[name] = pltpu.make_async_copy(src, dst, wsem.at[i])
        loads[name].start()
    barrier = entry_barrier(n_dev, me, everyone)

    sent = []

    def pair_of_sems(view):
        idx = 2 * len(sent)
        sent.append((view, sems.at[idx]))
        return sems.at[idx], sems.at[idx + 1]

    def start(src_of, dst, n, at, coords):
        view = dst.at[pl.ds(0, n - 1)]
        send_sem, recv_sem = pair_of_sems(view)
        spread(src_of, dst, n, at, coords, send_sem, recv_sem)
        return lambda: wait_for(view, recv_sem)

    def to_partner(src, dst):
        send_sem, recv_sem = pair_of_sems(dst)
        pltpu.make_async_remote_copy(
            src_ref=src, dst_ref=dst, send_sem=send_sem, recv_sem=recv_sem,
            device_id=(2 * ring_at + 1 - core, row, col), device_id_type=MESH,
        ).start()
        return lambda: wait_for(dst, recv_sem)

    def vis_begin(part, pair):
        return to_partner(part.at[1 - core], pair)

    def vis_middle(arrived, part, pair, ring):
        arrived()
        ring[ring_at] = (part[core].astype(F32) + pair[...].astype(F32)).astype(BF)
        return start(lambda p: ring.at[ring_at], ring, n_ring, ring_at, in_ring)

    def vis_finish(arrived, ring, result):
        arrived()
        value = ring[0].astype(F32)
        for i in range(1, n_ring):
            value = value + ring[i].astype(F32)
        result[core] = value.astype(BF)
        return to_partner(result.at[core], result.at[core])

    def fill(part, value, n, chunk):
        for i in range(n):
            part[i] = value[i * chunk:(i + 1) * chunk].astype(BF)

    def total(recv, part, n, at):
        recv[at] = part[at]
        result = recv[0].astype(F32)
        for i in range(1, n):
            result = result + recv[i].astype(F32)
        return result

    def whole(buf, n):
        return jnp.concatenate([buf[i].astype(F32) for i in range(n)], axis=0)

    values = images[...].astype(F32)
    centred = values - jnp.mean(values, axis=-1, keepdims=True)
    inverse_scale = lax.rsqrt(jnp.mean(centred * centred, axis=-1, keepdims=True) + 1e-05)
    normed = centred * inverse_scale * gain[...]
    for i in range(n_vis):
        blocks[i] = normed[:, i * vf:(i + 1) * vf].astype(BF)
    pl.semaphore_wait(barrier, n_dev - 1)
    cot_done = start(lambda p: cot, cot_all, group, pos, in_group)
    rows_done = start(lambda p: blocks.at[lax.rem(p, n_vis)], rows_all, n_dev, me, everyone)
    cot_all[pos] = cot[...]
    rows_all[me] = blocks[vis]

    cot_done()
    upstream[...] = whole(cot_all, group).astype(BF)
    loads["wd"].wait()
    for t in range(TILES):
        cols = slice(t * tw, (t + 1) * tw)
        value = dot_nt(upstream[...], wd[cols, :])
        for i in range(2):
            h_part[i, :, cols] = value[i * hr:(i + 1) * hr].astype(BF)
    h_done = vis_begin(h_part, h_pair)
    n_slots = n_dev * per
    place = row_places(counts, order, n_vis, per, (rows, n_slots), 1)
    pick = jnp.where(place == lax.broadcasted_iota(jnp.int32, (rows, n_slots), 0), 1.0, 0.0).astype(BF)

    loads["wf"].wait()
    rows_done()
    packed_out[...] = jnp.dot(
        pick, rows_all[...].reshape(n_slots, vf), preferred_element_type=F32
    ).astype(BF)
    fill(b_part, jnp.dot(packed_out[...], wf[...], preferred_element_type=F32), 2, hr)
    b_done = vis_begin(b_part, b_pair)
    b_done = vis_middle(b_done, b_part, b_pair, b_ring)
    h_done = vis_middle(h_done, h_part, h_pair, h_ring)
    b_done = vis_finish(b_done, b_ring, b_all)
    b_done()
    pre = whole(b_all, 2) + bias[...]
    activated, slope_value = gelu_parts(pre)
    slope[...] = slope_value
    hid_out[...] = activated.astype(BF)

    loads["ws"].wait()
    fill(c_part, jnp.dot(hid_out[...], ws[...], preferred_element_type=F32), group, gr)
    c_done = start(lambda p: c_part.at[p], c_recv, group, pos, in_group)
    h_done = vis_finish(h_done, h_ring, h_all)
    c_done()
    c_all[pos] = total(c_recv, c_part, group, pos).astype(BF)
    c_done = start(lambda p: c_all.at[pos], c_all, group, pos, in_group)
    loads["wg"].wait()
    loads["wu"].wait()
    h_done()
    c_done()
    inputs[...] = whole(c_all, group).astype(BF)

    d_done = [None] * TILES
    for t in range(TILES):
        cols = slice(t * tw, (t + 1) * tw)
        for half, weight in enumerate((wg, wu)):
            value = jnp.dot(inputs[...], weight[:, cols], preferred_element_type=F32)
            for i in range(2):
                d_part[t, i, :, half * tw:(half + 1) * tw] = value[i * hr:(i + 1) * hr].astype(BF)
        d_done[t] = vis_begin(d_part.at[t], d_pair.at[t])
        if t > 0:
            d_done[t - 1] = vis_middle(d_done[t - 1], d_part.at[t - 1], d_pair.at[t - 1], d_ring.at[t - 1])
    d_done[-1] = vis_middle(d_done[-1], d_part.at[TILES - 1], d_pair.at[TILES - 1], d_ring.at[TILES - 1])
    d_done[0] = vis_finish(d_done[0], d_ring.at[0], d_all.at[0])
    for t in range(TILES):
        if t + 1 < TILES:
            d_done[t + 1] = vis_finish(d_done[t + 1], d_ring.at[t + 1], d_all.at[t + 1])
        d_done[t]()
        cols = slice(t * tw, (t + 1) * tw)
        both = whole(d_all.at[t], 2)
        gate_sum, up_sum = both[:, :tw], both[:, tw:]
        hidden_grad = jnp.concatenate([h_all[i, :, cols].astype(F32) for i in range(2)], axis=0)
        gate_sigmoid = jax.nn.sigmoid(gate_sum)
        hidden[:, cols] = (gate_sum * gate_sigmoid * up_sum).astype(BF)
        gate_grad, up_grad = feed_grads(hidden_grad, gate_sum, up_sum, gate_sigmoid)
        value = dot_nt(gate_grad, wg[:, cols]) + dot_nt(up_grad, wu[:, cols])
        if t == 0:
            acc[...] = value
        else:
            acc[...] += value
    fill(e_part, acc[...], group, gr)
    e_done = start(lambda p: e_part.at[p], e_recv, group, pos, in_group)

    fill(o_part, jnp.dot(hidden[...], wd[...], preferred_element_type=F32), group, gr)
    e_done()
    e_all[pos] = (total(e_recv, e_part, group, pos) + cot[...].astype(F32)).astype(BF)
    e_done = start(lambda p: e_all.at[pos], e_all, group, pos, in_group)
    o_done = start(lambda p: o_part.at[p], o_recv, group, pos, in_group)
    place = row_places(counts, order, n_vis, per, (n_slots, rows), 0)
    put = jnp.where(place == lax.broadcasted_iota(jnp.int32, (n_slots, rows), 1), 1.0, 0.0).astype(BF)
    e_done()
    ig_out[...] = whole(e_all, group).astype(BF)
    fill(f_part, dot_nt(ig_out[...], ws[...]), 2, hr)
    f_done = vis_begin(f_part, f_pair)
    f_done = vis_middle(f_done, f_part, f_pair, f_ring)
    o_done()
    block_out[...] = (c_all[pos].astype(F32) + total(o_recv, o_part, group, pos)).astype(BF)
    f_done = vis_finish(f_done, f_ring, f_all)
    f_done()
    act_out[...] = (whole(f_all, 2) * slope[...]).astype(BF)

    slot_act = jnp.dot(put, act_out[...], preferred_element_type=F32).astype(BF)
    slabs[...] = dot_nt(slot_act, wf[...]).astype(BF).reshape(n_dev, per, vf)
    slabs_done = start(lambda p: slabs.at[p], slabs_recv, n_dev, me, everyone)
    slabs_recv[me] = slabs[me]
    slabs_done()
    pieces = []
    for i in range(n_vis):
        value = slabs_recv[i].astype(F32)
        for g in range(1, group):
            value = value + slabs_recv[g * n_vis + i].astype(F32)
        pieces.append(value)
    standardized_input = centred * inverse_scale
    slot_out[...] = norm_gradient_pass(
        jnp.concatenate(pieces, axis=1), standardized_input, inverse_scale, gain[...]
    )
    for view, sem in sent:
        wait_for(view, sem)


def vis_buffers(n_vis, lead, half_rows, width):
    return [
        pltpu.VMEM(lead + (2, half_rows, width), BF),
        pltpu.VMEM(lead + (half_rows, width), BF),
        pltpu.VMEM(lead + (n_vis // 2, half_rows, width), BF),
        pltpu.VMEM(lead + (2, half_rows, width), BF),
    ]


def on_device(
    sizes,
    images,
    counts,
    block_order,
    projector_norm_gain,
    proj_first,
    proj_bias,
    proj_second,
    gate_weight,
    up_weight,
    down_weight,
    cotangent,
):
    n_vis, n_row, n_col = sizes
    group_size = n_row * n_col
    n_dev = n_vis * group_size
    per_device = images.shape[0]
    local_rows = cotangent.shape[0]
    rows = local_rows * group_size
    vf, units = proj_first.shape
    dl, ffl = gate_weight.shape
    hr = rows // 2
    by_group = pltpu.VMEM((group_size, local_rows, dl), BF)
    by_device = pltpu.VMEM((n_dev, per_device, vf), BF)
    sm = pl.BlockSpec(memory_space=pltpu.SMEM)
    n_sends = 3 * (3 + TILES) + 5 + 3
    block_out, image_slot_gradients, packed, act_grad, hidden_proj, input_grad = pl.pallas_call(
        functools.partial(chain_kernel, sizes),
        out_shape=(
            jax.ShapeDtypeStruct((local_rows, dl), BF),
            jax.ShapeDtypeStruct(images.shape, F32),
            jax.ShapeDtypeStruct((rows, vf), BF),
            jax.ShapeDtypeStruct((rows, units), BF),
            jax.ShapeDtypeStruct((rows, units), BF),
            jax.ShapeDtypeStruct((rows, dl), BF),
        ),
        in_specs=[sm, sm, VM, VM, VM, VM, ANY, ANY, ANY, ANY, ANY],
        out_specs=(VM,) * 6,
        scratch_shapes=[
            pltpu.VMEM(proj_first.shape, BF),
            pltpu.VMEM(proj_second.shape, BF),
            pltpu.VMEM(gate_weight.shape, BF),
            pltpu.VMEM(up_weight.shape, BF),
            pltpu.VMEM(down_weight.shape, BF),
            pltpu.VMEM((n_vis, per_device, vf), BF),
            by_device,
            by_group,
            pltpu.VMEM((rows, dl), BF),
            by_device,
            by_device,
            *vis_buffers(n_vis, (), hr, units),
            *vis_buffers(n_vis, (), hr, ffl),
            *vis_buffers(n_vis, (TILES,), hr, 2 * ffl // TILES),
            *vis_buffers(n_vis, (), hr, units),
            *[by_group] * 8,
            pltpu.VMEM((rows, units), F32),
            pltpu.VMEM((rows, dl), BF),
            pltpu.VMEM((rows, dl), F32),
            pltpu.VMEM((rows, ffl), BF),
            pltpu.SemaphoreType.DMA((5,)),
            pltpu.SemaphoreType.DMA((2 * n_sends,)),
        ],
        compiler_params=pltpu.CompilerParams(
            collective_id=0, has_side_effects=True, vmem_limit_bytes=48 << 20
        ),
    )(
        counts, block_order, images, projector_norm_gain[None, :], cotangent,
        proj_bias[None, :], proj_first, proj_second, gate_weight, up_weight, down_weight,
    )
    second_grad = product(hidden_proj.T, input_grad)
    first_grad = product(packed.T, act_grad)
    return (block_out, image_slot_gradients, first_grad, second_grad)


def solution(mesh):
    in_specs = (
        P(("vis", "row", "col"), None),
        P(),
        P(),
        P(),
        P("vis", ("row", "col")),
        P(("row", "col")),
        P(("row", "col"), "vis"),
        P("vis", ("row", "col")),
        P("vis", ("row", "col")),
        P(("row", "col"), "vis"),
        P(("row", "col"), "vis"),
    )
    out_specs = (
        P(("row", "col"), "vis"),
        P(("vis", "row", "col"), None),
        P("vis", ("row", "col")),
        P(("row", "col"), "vis"),
    )
    sizes = (mesh.shape["vis"], mesh.shape["row"], mesh.shape["col"])
    return jax.shard_map(
        functools.partial(on_device, sizes), mesh=mesh, in_specs=in_specs, out_specs=out_specs, check_vma=False
    )
```

time: 105 us -> 88.2 us (0.84)
  the two profiles are of different devices: /device:TPU:0 before, /device:TPU:29 now
where the time goes in v2:
time: 88.2 us; the launch traced here: 87.8 us
  Pallas kernels  74.9 us (85%)
  local copies, waits for them, and re-layouts  8.17 us (9%)
  matrix products  4.09 us (5%)
    pallas_call x1, Pallas kernels, on_device(): pl.pallas_call(functools.partial(chain_kernel, sizes), out_shape=(jax.Sha...  74.9 us
    unnamed x16, local copies, waits for them, and re-layouts  7.41 us
    dot_general x2, matrix products, product(): return jnp.dot(left, right, preferred_element_type=jnp.float32)  4.09 us

profile of v2, /device:TPU:29, one launch (start us, length us, event | category | flops | bytes accessed | tf_op | source)
XLA Modules:
  0.0 87.8 jit_solution(10947369022073551836)
XLA Ops:
  0.6 0.8 broadcast_in_dim.6.gain
  1.4 0.0 copy-start
  1.4 1.4 %copy-done = bf16[1600,512]{1,0:T(8,128)(2,1)S(1)} copy-done((bf16[1600,512]{1,0:T(8,128)(2,1)S(1)}, bf16[1600,512]{1,0:T(8,128)(2,1)}, u32[]{:S(2)}) %copy-start) | copy-done | bytes 1638424
  2.8 0.0 copy-start.1
  2.8 1.2 %copy-done.1 = bf16[512,1024]{1,0:T(8,128)(2,1)S(1)} copy-done((bf16[512,1024]{1,0:T(8,128)(2,1)S(1)}, bf16[512,1024]{1,0:T(8,128)(2,1)}, u32[]{:S(2)}) %copy-start.1) | copy-done | bytes 1048600
  4.1 0.0 copy-start.2
  4.1 0.8 copy-done.2
  4.9 0.0 copy-start.3
  4.9 0.7 copy-done.3
  5.6 0.0 copy-start.4
  5.6 0.7 copy-done.4
  6.3 0.0 copy-start.5
  6.3 0.7 copy-done.5
  6.9 0.0 copy-start.6
  6.9 0.7 copy-done.6
  7.6 74.9 %shard_map.138 = (bf16[8,1024]{1,0:T(8,128)(2,1)S(1)}, f32[4,6400]{1,0:T(4,128)S(1)}, bf16[64,1600]{1,0:T(8,128)(2,1)S(1)}, bf16[64,512]{1,0:T(8,128)(2,1)S(1)},...) custom-call(s32[4]{0:T(128)S(1)} %copy-done.5, s32[4]{0:T(128)S(1)} %copy-done.6, ...), custom_call_target="tpu_custom_call" | custom-call | tf_op jit(solution)/shard_map/pallas_call | solution.py:358
  82.5 2.3 %fusion = f32[1600,512]{1,0:T(8,128)} fusion(bf16[64,1600]{1,0:T(8,128)(2,1)S(1)} %get-tuple-element.12, bf16[64,512]{1,0:T(8,128)(2,1)S(1)} %get-tuple-element.13), kind=kOutput, calls=%fused_computation | convolution fusion | flops 104857600 | bytes 3547136 | tf_op jit(solution)/shard_map/dot_general | solution.py:27
  84.8 1.8 %fusion.1 = f32[512,1024]{1,0:T(8,128)} fusion(bf16[64,512]{1,0:T(8,128)(2,1)S(1)} %get-tuple-element.14, bf16[64,1024]{1,0:T(8,128)(2,1)S(1)} %get-tuple-element.15), kind=kOutput, calls=%fused_computation.1 | convolution fusion | flops 67108864 | bytes 2293760 | tf_op jit(solution)/shard_map/dot_general | solution.py:27
  86.6 0.6 copy.17
  87.2 0.6 copy.18
Async XLA Ops:
  1.4 1.4 %copy-start = (bf16[1600,512]{1,0:T(8,128)(2,1)S(1)}, bf16[1600,512]{1,0:T(8,128)(2,1)}, u32[]{:S(2)}) copy-start(bf16[1600,512]{1,0:T(8,128)(2,1)} %wf_hbm.1) | copy-start | bytes 4915204
  2.8 1.2 %copy-start.1 = (bf16[512,1024]{1,0:T(8,128)(2,1)S(1)}, bf16[512,1024]{1,0:T(8,128)(2,1)}, u32[]{:S(2)}) copy-start(bf16[512,1024]{1,0:T(8,128)(2,1)} %ws_hbm.1) | copy-start | bytes 3145732
  4.1 0.8 copy-start.2
  4.9 0.7 copy-start.3
  5.6 0.7 copy-start.4
  6.3 0.7 copy-start.5
  6.9 0.7 copy-start.6

commit v3 on v2

--- a/solution.py
+++ b/solution.py
@@ -60,12 +60,12 @@
     return barrier
 
 
-def spread(src_of, dst, n, me, coords, send_sem, recv_sem):
+def spread(src_of, dst, n, me, coords, send_sem, recv_sem, slab=None):
     def body(k, carry):
         p = lax.rem(me + k, n)
         pltpu.make_async_remote_copy(
             src_ref=src_of(p),
-            dst_ref=dst.at[me],
+            dst_ref=dst.at[me if slab is None else slab],
             send_sem=send_sem,
             recv_sem=recv_sem,
             device_id=coords(p),
@@ -108,14 +108,15 @@
 
 
 def chain_kernel(
-    sizes, counts, order, images, gain, cot, bias, wf_hbm, ws_hbm, wg_hbm, wu_hbm, wd_hbm,
+    sizes, counts_hbm, order_hbm, images_hbm, gain_hbm, cot_hbm, bias_hbm,
+    wf_hbm, ws_hbm, wg_hbm, wu_hbm, wd_hbm,
     block_out, slot_out, packed_out, act_out, hid_out, ig_out,
-    wf, ws, wg, wu, wd,
-    blocks, rows_all, cot_all, upstream, slabs, slabs_recv,
+    counts, order, images, gain, cot, bias, wf, ws, wg, wu, wd,
+    blocks, rows_all, cot_all, upstream, slabs, across, column_sums, returned,
     b_part, b_pair, b_ring, b_all, h_part, h_pair, h_ring, h_all,
     d_part, d_pair, d_ring, d_all, f_part, f_pair, f_ring, f_all,
     c_part, c_recv, c_all, e_part, e_recv, e_all, o_part, o_recv,
-    slope, inputs, acc, hidden, wsem, sems,
+    slope, inputs, acc, hidden, wsem, gather_sems, return_sems, sems,
 ):
     n_vis, n_row, n_col = sizes
     group = n_row * n_col
@@ -135,12 +136,19 @@
     def in_ring(p):
         return (2 * p + core, row, col)
 
+    def in_column(p):
+        return (lax.rem(p, n_vis), p // n_vis, col)
+
     def in_group(p):
         return (vis, p // n_col, p % n_col)
 
     loads = {}
     for i, (name, src, dst) in enumerate(
-        (("wd", wd_hbm, wd), ("wf", wf_hbm, wf), ("ws", ws_hbm, ws), ("wg", wg_hbm, wg), ("wu", wu_hbm, wu))
+        (
+            ("images", images_hbm, images), ("gain", gain_hbm, gain), ("cot", cot_hbm, cot),
+            ("bias", bias_hbm, bias), ("counts", counts_hbm, counts), ("order", order_hbm, order),
+            ("wd", wd_hbm, wd), ("wf", wf_hbm, wf), ("ws", ws_hbm, ws), ("wg", wg_hbm, wg), ("wu", wu_hbm, wu),
+        )
     ):
         loads[name] = pltpu.make_async_copy(src, dst, wsem.at[i])
         loads[name].start()
@@ -197,33 +205,62 @@
     def whole(buf, n):
         return jnp.concatenate([buf[i].astype(F32) for i in range(n)], axis=0)
 
+    loads["images"].wait()
+    loads["gain"].wait()
+    gain_row = gain[...].reshape(1, gain.shape[0])
     values = images[...].astype(F32)
     centred = values - jnp.mean(values, axis=-1, keepdims=True)
     inverse_scale = lax.rsqrt(jnp.mean(centred * centred, axis=-1, keepdims=True) + 1e-05)
-    normed = centred * inverse_scale * gain[...]
+    normed = centred * inverse_scale * gain_row
     for i in range(n_vis):
         blocks[i] = normed[:, i * vf:(i + 1) * vf].astype(BF)
+    for name in ("cot", "bias", "counts", "order"):
+        loads[name].wait()
     pl.semaphore_wait(barrier, n_dev - 1)
     cot_done = start(lambda p: cot, cot_all, group, pos, in_group)
-    rows_done = start(lambda p: blocks.at[lax.rem(p, n_vis)], rows_all, n_dev, me, everyone)
+    mates, own = n_row * n_vis, row * n_vis + vis
+    row_steps = sorted(range(n_row), key=lambda k: min(k, n_row - k))
+    mates_view = rows_all.at[pl.ds(0, mates - 1)]
+    send_sem, _ = pair_of_sems(mates_view)
+    spread(
+        lambda p: blocks.at[lax.rem(p, n_vis)], rows_all, mates, own, in_column,
+        send_sem, gather_sems.at[row], slab=me,
+    )
     cot_all[pos] = cot[...]
     rows_all[me] = blocks[vis]
+    forward_view = rows_all.at[pl.ds(0, mates * (n_col - 1))]
+    forward_send, forward_recv = pair_of_sems(forward_view)
+
+    def forward(k):
+        r = lax.rem(row + k, n_row)
+        wait_for(rows_all.at[pl.ds(0, n_vis - 1 if k == 0 else n_vis)], gather_sems.at[r])
+        chunk = rows_all.at[pl.ds((r * n_col + col) * n_vis, n_vis)]
+        for j in range(1, n_col):
+            pltpu.make_async_remote_copy(
+                src_ref=chunk, dst_ref=chunk, send_sem=forward_send, recv_sem=forward_recv,
+                device_id=(vis, row, lax.rem(col + j, n_col)), device_id_type=MESH,
+            ).start()
 
     cot_done()
     upstream[...] = whole(cot_all, group).astype(BF)
     loads["wd"].wait()
+    steps_left = list(row_steps)
     for t in range(TILES):
+        if steps_left:
+            forward(steps_left.pop(0))
         cols = slice(t * tw, (t + 1) * tw)
         value = dot_nt(upstream[...], wd[cols, :])
         for i in range(2):
             h_part[i, :, cols] = value[i * hr:(i + 1) * hr].astype(BF)
+    for k in steps_left:
+        forward(k)
     h_done = vis_begin(h_part, h_pair)
     n_slots = n_dev * per
     place = row_places(counts, order, n_vis, per, (rows, n_slots), 1)
     pick = jnp.where(place == lax.broadcasted_iota(jnp.int32, (rows, n_slots), 0), 1.0, 0.0).astype(BF)
 
     loads["wf"].wait()
-    rows_done()
+    wait_for(forward_view, forward_recv)
     packed_out[...] = jnp.dot(
         pick, rows_all[...].reshape(n_slots, vf), preferred_element_type=F32
     ).astype(BF)
@@ -233,7 +270,7 @@
     h_done = vis_middle(h_done, h_part, h_pair, h_ring)
     b_done = vis_finish(b_done, b_ring, b_all)
     b_done()
-    pre = whole(b_all, 2) + bias[...]
+    pre = whole(b_all, 2) + bias[...].reshape(1, bias.shape[0])
     activated, slope_value = gelu_parts(pre)
     slope[...] = slope_value
     hid_out[...] = activated.astype(BF)
@@ -302,18 +339,45 @@
 
     slot_act = jnp.dot(put, act_out[...], preferred_element_type=F32).astype(BF)
     slabs[...] = dot_nt(slot_act, wf[...]).astype(BF).reshape(n_dev, per, vf)
-    slabs_done = start(lambda p: slabs.at[p], slabs_recv, n_dev, me, everyone)
-    slabs_recv[me] = slabs[me]
-    slabs_done()
+    across_send, _ = pair_of_sems(slabs.at[pl.ds(0, mates * (n_col - 1))])
+    returned_view = returned.at[pl.ds(0, mates - 1)]
+    back_send, back_recv = pair_of_sems(returned_view)
+    back_steps = row_steps[::-1]
+    for k in back_steps:
+        r = lax.rem(row + k, n_row)
+        for j in range(1, n_col):
+            other = lax.rem(col + j, n_col)
+            pltpu.make_async_remote_copy(
+                src_ref=slabs.at[pl.ds((r * n_col + other) * n_vis, n_vis)],
+                dst_ref=across.at[r, col], send_sem=across_send, recv_sem=return_sems.at[r],
+                device_id=(vis, row, other), device_id_type=MESH,
+            ).start()
+    for k in back_steps:
+        r = lax.rem(row + k, n_row)
+        across[r, col] = slabs[pl.ds((r * n_col + col) * n_vis, n_vis)]
+        wait_for(across.at[0, pl.ds(0, n_col - 1)], return_sems.at[r])
+        value = across[r, 0].astype(F32)
+        for c in range(1, n_col):
+            value = value + across[r, c].astype(F32)
+        column_sums[r] = value.astype(BF)
+        for j in range(1 if k == 0 else 0, n_vis):
+            other = lax.rem(vis + j, n_vis)
+            pltpu.make_async_remote_copy(
+                src_ref=column_sums.at[r, other], dst_ref=returned.at[own],
+                send_sem=back_send, recv_sem=back_recv,
+                device_id=(other, r, col), device_id_type=MESH,
+            ).start()
+    returned[own] = column_sums[row, vis]
+    wait_for(returned_view, back_recv)
     pieces = []
     for i in range(n_vis):
-        value = slabs_recv[i].astype(F32)
-        for g in range(1, group):
-            value = value + slabs_recv[g * n_vis + i].astype(F32)
+        value = returned[i].astype(F32)
+        for r in range(1, n_row):
+            value = value + returned[r * n_vis + i].astype(F32)
         pieces.append(value)
     standardized_input = centred * inverse_scale
     slot_out[...] = norm_gradient_pass(
-        jnp.concatenate(pieces, axis=1), standardized_input, inverse_scale, gain[...]
+        jnp.concatenate(pieces, axis=1), standardized_input, inverse_scale, gain_row
     )
     for view, sem in sent:
         wait_for(view, sem)
@@ -353,8 +417,7 @@
     hr = rows // 2
     by_group = pltpu.VMEM((group_size, local_rows, dl), BF)
     by_device = pltpu.VMEM((n_dev, per_device, vf), BF)
-    sm = pl.BlockSpec(memory_space=pltpu.SMEM)
-    n_sends = 3 * (3 + TILES) + 5 + 3
+    n_sends = 3 * (3 + TILES) + 5 + 5
     block_out, image_slot_gradients, packed, act_grad, hidden_proj, input_grad = pl.pallas_call(
         functools.partial(chain_kernel, sizes),
         out_shape=(
@@ -365,9 +428,15 @@
             jax.ShapeDtypeStruct((rows, units), BF),
             jax.ShapeDtypeStruct((rows, dl), BF),
         ),
-        in_specs=[sm, sm, VM, VM, VM, VM, ANY, ANY, ANY, ANY, ANY],
+        in_specs=[ANY] * 11,
         out_specs=(VM,) * 6,
         scratch_shapes=[
+            pltpu.SMEM(counts.shape, jnp.int32),
+            pltpu.SMEM(block_order.shape, jnp.int32),
+            pltpu.VMEM(images.shape, BF),
+            pltpu.VMEM(projector_norm_gain.shape, F32),
+            pltpu.VMEM(cotangent.shape, BF),
+            pltpu.VMEM(proj_bias.shape, F32),
             pltpu.VMEM(proj_first.shape, BF),
             pltpu.VMEM(proj_second.shape, BF),
             pltpu.VMEM(gate_weight.shape, BF),
@@ -378,7 +447,9 @@
             by_group,
             pltpu.VMEM((rows, dl), BF),
             by_device,
-            by_device,
+            pltpu.VMEM((n_row, n_col, n_vis, per_device, vf), BF),
+            pltpu.VMEM((n_row, n_vis, per_device, vf), BF),
+            pltpu.VMEM((n_row * n_vis, per_device, vf), BF),
             *vis_buffers(n_vis, (), hr, units),
             *vis_buffers(n_vis, (), hr, ffl),
             *vis_buffers(n_vis, (TILES,), hr, 2 * ffl // TILES),
@@ -388,15 +459,17 @@
             pltpu.VMEM((rows, dl), BF),
             pltpu.VMEM((rows, dl), F32),
             pltpu.VMEM((rows, ffl), BF),
-            pltpu.SemaphoreType.DMA((5,)),
+            pltpu.SemaphoreType.DMA((11,)),
+            pltpu.SemaphoreType.DMA((n_row,)),
+            pltpu.SemaphoreType.DMA((n_row,)),
             pltpu.SemaphoreType.DMA((2 * n_sends,)),
         ],
         compiler_params=pltpu.CompilerParams(
             collective_id=0, has_side_effects=True, vmem_limit_bytes=48 << 20
         ),
     )(
-        counts, block_order, images, projector_norm_gain[None, :], cotangent,
-        proj_bias[None, :], proj_first, proj_second, gate_weight, up_weight, down_weight,
+        counts, block_order, images, projector_norm_gain, cotangent,
+        proj_bias, proj_first, proj_second, gate_weight, up_weight, down_weight,
     )
     second_grad = product(hidden_proj.T, input_grad)
     first_grad = product(packed.T, act_grad)

time: 88.2 us -> 87.9 us (level)
  the two profiles are of different devices: /device:TPU:29 before, /device:TPU:0 now
where the time goes in v3:
time: 87.9 us; the launch traced here: 87.5 us
  Pallas kernels  74.6 us (85%)
  local copies, waits for them, and re-layouts  8.15 us (9%)
  matrix products  4.1 us (5%)
    pallas_call x1, Pallas kernels, on_device(): pl.pallas_call(functools.partial(chain_kernel, sizes), out_shape=(jax.Sha...  74.6 us
    unnamed x18, local copies, waits for them, and re-layouts  8.15 us
    dot_general x2, matrix products, product(): return jnp.dot(left, right, preferred_element_type=jnp.float32)  4.1 us

profile of v3, /device:TPU:0, one launch (start us, length us, event | category | flops | bytes accessed | tf_op | source)
XLA Modules:
  0.0 87.5 jit_solution(11473250469374773868)
XLA Ops:
  0.6 0.0 copy-start
  0.6 1.4 %copy-done = bf16[1600,512]{1,0:T(8,128)(2,1)S(1)} copy-done((bf16[1600,512]{1,0:T(8,128)(2,1)S(1)}, bf16[1600,512]{1,0:T(8,128)(2,1)}, u32[]{:S(2)}) %copy-start) | copy-done | bytes 1638424
  2.1 0.0 copy-start.1
  2.1 1.2 %copy-done.1 = bf16[512,1024]{1,0:T(8,128)(2,1)S(1)} copy-done((bf16[512,1024]{1,0:T(8,128)(2,1)S(1)}, bf16[512,1024]{1,0:T(8,128)(2,1)}, u32[]{:S(2)}) %copy-start.1) | copy-done | bytes 1048600
  3.3 0.0 copy-start.2
  3.3 0.8 copy-done.2
  4.1 0.0 copy-start.3
  4.1 0.7 copy-done.3
  4.8 0.0 copy-start.4
  4.8 0.7 copy-done.4
  5.6 0.0 copy-start.5
  5.6 0.7 copy-done.5
  6.2 0.0 copy-start.6
  6.2 0.7 copy-done.6
  6.9 0.0 copy-start.7
  6.9 0.7 copy-done.7
  7.6 74.6 %shard_map.138 = (bf16[8,1024]{1,0:T(8,128)(2,1)S(1)}, f32[4,6400]{1,0:T(4,128)S(1)}, bf16[64,1600]{1,0:T(8,128)(2,1)S(1)}, bf16[64,512]{1,0:T(8,128)(2,1)S(1)},...) custom-call(s32[4]{0:T(128)S(1)} %copy-done.6, s32[4]{0:T(128)S(1)} %copy-done.7, ...), custom_call_target="tpu_custom_call" | custom-call | tf_op jit(solution)/shard_map/pallas_call | solution.py:421
  82.2 2.3 %fusion = f32[1600,512]{1,0:T(8,128)} fusion(bf16[64,1600]{1,0:T(8,128)(2,1)S(1)} %get-tuple-element.12, bf16[64,512]{1,0:T(8,128)(2,1)S(1)} %get-tuple-element.13), kind=kOutput, calls=%fused_computation | convolution fusion | flops 104857600 | bytes 3547136 | tf_op jit(solution)/shard_map/dot_general | solution.py:27
  84.5 1.8 %fusion.1 = f32[512,1024]{1,0:T(8,128)} fusion(bf16[64,512]{1,0:T(8,128)(2,1)S(1)} %get-tuple-element.14, bf16[64,1024]{1,0:T(8,128)(2,1)S(1)} %get-tuple-element.15), kind=kOutput, calls=%fused_computation.1 | convolution fusion | flops 67108864 | bytes 2293760 | tf_op jit(solution)/shard_map/dot_general | solution.py:27
  86.3 0.6 copy.17
  86.9 0.6 copy.18
Async XLA Ops:
  0.6 1.4 %copy-start = (bf16[1600,512]{1,0:T(8,128)(2,1)S(1)}, bf16[1600,512]{1,0:T(8,128)(2,1)}, u32[]{:S(2)}) copy-start(bf16[1600,512]{1,0:T(8,128)(2,1)} %wf_hbm.1) | copy-start | bytes 4915204
  2.1 1.2 %copy-start.1 = (bf16[512,1024]{1,0:T(8,128)(2,1)S(1)}, bf16[512,1024]{1,0:T(8,128)(2,1)}, u32[]{:S(2)}) copy-start(bf16[512,1024]{1,0:T(8,128)(2,1)} %ws_hbm.1) | copy-start | bytes 3145732
  3.3 0.8 copy-start.2
  4.1 0.7 copy-start.3
  4.8 0.7 copy-start.4
  5.6 0.7 copy-start.5
  6.2 0.7 copy-start.6
  6.9 0.7 copy-start.7
